TPU v7x, 32 devices: a whole 2x2x4 slice. The times are simulated.
32 devices in a mesh: dp: 8 (over z, y), tensor: 4 (over x, core).
Axes of the slice: x: 2, y: 2, z: 4, core: 2. Of those that a mesh axis runs over, the one named last changes fastest.
Arguments:
- tokens: bfloat16 [16384, 768], P(('dp', 'tensor')), may hold values from -6 to 6
- segments: int32 [8, 2048], P('dp', 'tensor'), may hold values from 0 to 3, never falling along the last dimension, each value on 1 to 1024 neighbouring positions
- query_proj: bfloat16 [768, 768], P('dp', 'tensor'), may hold values from -0.3125 to 0.3125
- query_bias: float32 [768], P(('dp', 'tensor')), may hold values from -3 to 3
- key_proj: bfloat16 [768, 768], P('dp', 'tensor'), may hold values from -0.21875 to 0.21875
- value_proj: bfloat16 [768, 768], P('dp', 'tensor'), may hold values from -0.21875 to 0.21875
- value_bias: float32 [768], P(('dp', 'tensor')), may hold values from -3 to 3
- merge_proj: bfloat16 [768, 768], P('tensor', 'dp'), may hold values from -1.75 to 1.75
- merge_bias: float32 [768], P(('dp', 'tensor')), may hold values from -3 to 3
- first_gain: float32 [768], P(('dp', 'tensor')), may hold values from 0.5 to 1.5
- first_shift: float32 [768], P(('dp', 'tensor')), may hold values from -3 to 3
- expand_proj: bfloat16 [768, 3072], P('dp', 'tensor'), may hold values from -0.21875 to 0.21875
- expand_bias: float32 [3072], P(('dp', 'tensor')), may hold values from -3 to 3
- shrink_proj: bfloat16 [3072, 768], P('tensor', 'dp'), may hold values from -0.15625 to 0.15625
- shrink_bias: float32 [768], P(('dp', 'tensor')), may hold values from -3 to 3
- second_gain: float32 [768], P(('dp', 'tensor')), may hold values from 0.5 to 1.5
- second_shift: float32 [768], P(('dp', 'tensor')), may hold values from -3 to 3
- cotangent: bfloat16 [16384, 768], P(('dp', 'tensor')), may hold values from -6 to 6
Outputs:
- output: bfloat16 [16384, 768], P(('dp', 'tensor'))
- tokens_grad: bfloat16 [16384, 768], P(('dp', 'tensor'))
- querygrad: float32 [768, 768], P('dp', 'tensor')
- qbiasgrad: float32 [768], P(('dp', 'tensor'))
- keygrad: float32 [768, 768], P('dp', 'tensor')
- valuegrad: float32 [768, 768], P('dp', 'tensor')
- vbiasgrad: float32 [768], P(('dp', 'tensor'))
- mergegrad: float32 [768, 768], P('tensor', 'dp')
- mbiasgrad: float32 [768], P(('dp', 'tensor'))
- fgaingrad: float32 [768], P(('dp', 'tensor'))
- fshiftgrad: float32 [768], P(('dp', 'tensor'))
- expandgrad: float32 [768, 3072], P('dp', 'tensor')
- ebiasgrad: float32 [3072], P(('dp', 'tensor'))
- shrinkgrad: float32 [3072, 768], P('tensor', 'dp')
- sbiasgrad: float32 [768], P(('dp', 'tensor'))
- sgaingrad: float32 [768], P(('dp', 'tensor'))
- sshiftgrad: float32 [768], P(('dp', 'tensor'))
Inputs may be any that keep to these rules, and one draw needn't show every extreme that they name: `segments`: along each sequence the segment numbers never fall; each of the 4 numbers marks 1 to 1024 positions of every sequence.
All inputs are finite; a program needn't handle non-finite values.
Results may differ from a plain program's by a relative error of at most 0.023.
Values may be sent and summed in bfloat16 or wider, within the bound.
No kernel may reach another device: no remote copies, remote signals or barrier semaphores. Data moves between devices by JAX's collectives and lax.ppermute only.
A program may use at most 128 MiB of HBM per device.

v0:
```python
import jax
import jax.numpy as jnp
from jax import lax
from jax.sharding import PartitionSpec as P

HD = 64
EPSILON = 1e-12
CONTRACT_ROWS = (((0,), (0,)), ((), ()))
CONTRACT_COLUMNS = (((1,), (1,)), ((), ()))


def normalize(values, gain, shift):
    centre = jnp.mean(values, axis=-1, keepdims=True)
    centred = values - centre
    spread = jnp.mean(centred * centred, axis=-1, keepdims=True)
    return centred * lax.rsqrt(spread + EPSILON) * gain + shift


def gelu_exact(values):
    return jax.nn.gelu(values, approximate=False)


def assemble(pieces, count, heads):
    block = pieces.shape[1]
    depth = pieces.shape[2]
    return (
        pieces.reshape(count, heads, block, depth)
        .transpose(0, 2, 1, 3)
        .reshape(count * block, heads * depth)
    )


def attend(query, keys, values, seg_row, depth):
    length, width = query.shape
    heads = width // depth
    block = min(512, length)
    count = length // block
    scale = depth ** (-0.5)

    def one(index):
        start = index // heads * block
        column = index % heads * depth
        query_rows = lax.dynamic_slice(query, (start, column), (block, depth))
        key_head = lax.dynamic_slice(keys, (0, column), (length, depth))
        value_head = lax.dynamic_slice(values, (0, column), (length, depth))
        seg_rows = lax.dynamic_slice_in_dim(seg_row, start, block)
        scores = (
            lax.dot_general(
                query_rows, key_head, CONTRACT_COLUMNS, preferred_element_type=jnp.float32
            )
            * scale
        )
        scores = jnp.where(seg_rows[:, None] == seg_row[None, :], scores, -1e30)
        peak = jnp.max(scores, axis=1, keepdims=True)
        raised = jnp.exp(scores - peak)
        total = jnp.sum(raised, axis=1, keepdims=True)
        chance = (raised / total).astype(jnp.bfloat16)
        context = jnp.dot(chance, value_head, preferred_element_type=jnp.float32)
        return (context, (peak + jnp.log(total))[:, 0])

    contexts, logsum = lax.map(one, jnp.arange(count * heads))
    return (assemble(contexts, count, heads), logsum)


def attend_back(query, keys, values, grad_context, logsum, seg_row, depth):
    length, width = query.shape
    heads = width // depth
    block = min(512, length)
    count = length // block
    scale = depth ** (-0.5)

    def one(carry, index):
        grad_keys, grad_values = carry
        start = index // heads * block
        column = index % heads * depth
        query_rows = lax.dynamic_slice(query, (start, column), (block, depth))
        grad_rows = lax.dynamic_slice(grad_context, (start, column), (block, depth))
        key_head = lax.dynamic_slice(keys, (0, column), (length, depth))
        value_head = lax.dynamic_slice(values, (0, column), (length, depth))
        seg_rows = lax.dynamic_slice_in_dim(seg_row, start, block)
        scores = (
            lax.dot_general(
                query_rows, key_head, CONTRACT_COLUMNS, preferred_element_type=jnp.float32
            )
            * scale
        )
        scores = jnp.where(seg_rows[:, None] == seg_row[None, :], scores, -1e30)
        chance = jnp.exp(scores - logsum[index][:, None])
        grad_chance = lax.dot_general(
            grad_rows, value_head, CONTRACT_COLUMNS, preferred_element_type=jnp.float32
        )
        inner = jnp.sum(chance * grad_chance, axis=1, keepdims=True)
        grad_scores = (chance * (grad_chance - inner) * scale).astype(jnp.bfloat16)
        grad_query = jnp.dot(grad_scores, key_head, preferred_element_type=jnp.float32)
        key_part = lax.dot_general(
            grad_scores, query_rows, CONTRACT_ROWS, preferred_element_type=jnp.float32
        )
        value_part = lax.dot_general(
            chance.astype(jnp.bfloat16),
            grad_rows,
            CONTRACT_ROWS,
            preferred_element_type=jnp.float32,
        )
        old_keys = lax.dynamic_slice(grad_keys, (0, column), (length, depth))
        old_values = lax.dynamic_slice(grad_values, (0, column), (length, depth))
        grad_keys = lax.dynamic_update_slice(grad_keys, old_keys + key_part, (0, column))
        grad_values = lax.dynamic_update_slice(grad_values, old_values + value_part, (0, column))
        return ((grad_keys, grad_values), grad_query)

    empty = jnp.zeros((length, width), jnp.float32)
    (grad_keys, grad_values), grad_queries = lax.scan(
        one, (empty, empty), jnp.arange(count * heads)
    )
    return (assemble(grad_queries, count, heads), grad_keys, grad_values)


def widen(local, full_size, offset):
    return lax.dynamic_update_slice_in_dim(jnp.zeros((full_size,), jnp.float32), local, offset, 0)


def on_device(
    tokens,
    segments,
    query_proj,
    query_bias,
    key_proj,
    value_proj,
    value_bias,
    merge_proj,
    merge_bias,
    first_gain,
    first_shift,
    expand_proj,
    expand_bias,
    shrink_proj,
    shrink_bias,
    second_gain,
    second_shift,
    cotangent,
):
    part = lax.axis_index("tensor")
    query_full, key_full, value_full, merge_full, expand_full, shrink_full = (
        lax.all_gather(query_proj, "dp", axis=0, tiled=True),
        lax.all_gather(key_proj, "dp", axis=0, tiled=True),
        lax.all_gather(value_proj, "dp", axis=0, tiled=True),
        lax.all_gather(merge_proj, "dp", axis=1, tiled=True),
        lax.all_gather(expand_proj, "dp", axis=0, tiled=True),
        lax.all_gather(shrink_proj, "dp", axis=1, tiled=True),
    )
    (
        bias_query,
        bias_value,
        bias_merge,
        gain_first,
        shift_first,
        bias_expand,
        bias_shrink,
        gain_second,
        shift_second,
    ) = (
        lax.all_gather(query_bias, ("dp", "tensor"), axis=0, tiled=True),
        lax.all_gather(value_bias, ("dp", "tensor"), axis=0, tiled=True),
        lax.all_gather(merge_bias, ("dp", "tensor"), axis=0, tiled=True),
        lax.all_gather(first_gain, ("dp", "tensor"), axis=0, tiled=True),
        lax.all_gather(first_shift, ("dp", "tensor"), axis=0, tiled=True),
        lax.all_gather(expand_bias, ("dp", "tensor"), axis=0, tiled=True),
        lax.all_gather(shrink_bias, ("dp", "tensor"), axis=0, tiled=True),
        lax.all_gather(second_gain, ("dp", "tensor"), axis=0, tiled=True),
        lax.all_gather(second_shift, ("dp", "tensor"), axis=0, tiled=True),
    )
    width = query_full.shape[1]
    units = expand_full.shape[1]
    model_width = bias_query.shape[0]
    unit_count = bias_expand.shape[0]
    local_query_bias = lax.dynamic_slice_in_dim(bias_query, part * width, width)
    local_value_bias = lax.dynamic_slice_in_dim(bias_value, part * width, width)
    local_expand_bias = lax.dynamic_slice_in_dim(bias_expand, part * units, units)
    full_tokens, full_segments = (
        lax.all_gather(tokens, "tensor", axis=0, tiled=True),
        lax.all_gather(segments, "tensor", axis=1, tiled=True),
    )
    seg_row = full_segments[0]
    query = (
        jnp.dot(full_tokens, query_full, preferred_element_type=jnp.float32) + local_query_bias
    ).astype(jnp.bfloat16)
    keys = jnp.dot(full_tokens, key_full, preferred_element_type=jnp.float32).astype(jnp.bfloat16)
    values = (
        jnp.dot(full_tokens, value_full, preferred_element_type=jnp.float32) + local_value_bias
    ).astype(jnp.bfloat16)
    context, logsum = attend(query, keys, values, seg_row, HD)
    context_low = context.astype(jnp.bfloat16)
    attended = lax.psum_scatter(
        jnp.dot(context_low, merge_full, preferred_element_type=jnp.float32).astype(jnp.bfloat16),
        "tensor",
        scatter_dimension=0,
        tiled=True,
    ).astype(jnp.float32)
    mixed = tokens.astype(jnp.float32) + attended + bias_merge
    hidden = normalize(mixed, gain_first, shift_first)
    full_hidden = lax.all_gather(hidden.astype(jnp.bfloat16), "tensor", axis=0, tiled=True)
    inner = (
        jnp.dot(full_hidden, expand_full, preferred_element_type=jnp.float32) + local_expand_bias
    )
    active = gelu_exact(inner).astype(jnp.bfloat16)
    summed = (
        hidden
        + lax.psum_scatter(
            jnp.dot(active, shrink_full, preferred_element_type=jnp.float32).astype(jnp.bfloat16),
            "tensor",
            scatter_dimension=0,
            tiled=True,
        ).astype(jnp.float32)
        + bias_shrink
    )
    result, pull_second = jax.vjp(normalize, summed, gain_second, shift_second)
    output = result.astype(jnp.bfloat16)
    grad_summed, grad_gain_second, grad_shift_second = pull_second(cotangent.astype(jnp.float32))
    grad_bias_shrink = jnp.sum(grad_summed, axis=0)
    full_grad_summed = lax.all_gather(
        grad_summed.astype(jnp.bfloat16), "tensor", axis=0, tiled=True
    )
    shrink_local = lax.dot_general(
        active, full_grad_summed, CONTRACT_ROWS, preferred_element_type=jnp.float32
    )
    grad_active = lax.dot_general(
        full_grad_summed, shrink_full, CONTRACT_COLUMNS, preferred_element_type=jnp.float32
    )
    grad_inner = jax.vjp(gelu_exact, inner)[1](grad_active)[0]
    expand_bias_term = widen(jnp.sum(grad_inner, axis=0), unit_count, part * units)
    inner_low = grad_inner.astype(jnp.bfloat16)
    expand_local = lax.dot_general(
        full_hidden, inner_low, CONTRACT_ROWS, preferred_element_type=jnp.float32
    )
    grad_hidden = grad_summed + lax.psum_scatter(
        lax.dot_general(
            inner_low, expand_full, CONTRACT_COLUMNS, preferred_element_type=jnp.float32
        ).astype(jnp.bfloat16),
        "tensor",
        scatter_dimension=0,
        tiled=True,
    ).astype(jnp.float32)
    grad_mixed, grad_gain_first, grad_shift_first = jax.vjp(
        normalize, mixed, gain_first, shift_first
    )[1](grad_hidden)
    grad_bias_merge = jnp.sum(grad_mixed, axis=0)
    full_grad_mixed = lax.all_gather(grad_mixed.astype(jnp.bfloat16), "tensor", axis=0, tiled=True)
    merge_local = lax.dot_general(
        context_low, full_grad_mixed, CONTRACT_ROWS, preferred_element_type=jnp.float32
    )
    grad_context = lax.dot_general(
        full_grad_mixed, merge_full, CONTRACT_COLUMNS, preferred_element_type=jnp.float32
    ).astype(jnp.bfloat16)
    grad_query, grad_keys, grad_values = attend_back(
        query, keys, values, grad_context, logsum, seg_row, HD
    )
    grad_bias_query = jnp.sum(grad_query, axis=0)
    grad_bias_value = jnp.sum(grad_values, axis=0)
    query_low = grad_query.astype(jnp.bfloat16)
    key_low = grad_keys.astype(jnp.bfloat16)
    value_low = grad_values.astype(jnp.bfloat16)
    query_local = lax.dot_general(
        full_tokens, query_low, CONTRACT_ROWS, preferred_element_type=jnp.float32
    )
    key_local = lax.dot_general(
        full_tokens, key_low, CONTRACT_ROWS, preferred_element_type=jnp.float32
    )
    value_local = lax.dot_general(
        full_tokens, value_low, CONTRACT_ROWS, preferred_element_type=jnp.float32
    )
    total = lax.dot_general(
        query_low, query_full, CONTRACT_COLUMNS, preferred_element_type=jnp.float32
    )
    total = total + lax.dot_general(
        key_low, key_full, CONTRACT_COLUMNS, preferred_element_type=jnp.float32
    )
    tokens_grad = (
        grad_mixed
        + lax.psum_scatter(
            (
                total
                + lax.dot_general(
                    value_low, value_full, CONTRACT_COLUMNS, preferred_element_type=jnp.float32
                )
            ).astype(jnp.bfloat16),
            "tensor",
            scatter_dimension=0,
            tiled=True,
        ).astype(jnp.float32)
    ).astype(jnp.bfloat16)
    (
        qbiasgrad,
        vbiasgrad,
        mbiasgrad,
        fgaingrad,
        fshiftgrad,
        ebiasgrad,
        sbiasgrad,
        sgaingrad,
        sshiftgrad,
    ) = (
        lax.psum_scatter(
            widen(grad_bias_query, model_width, part * width),
            ("dp", "tensor"),
            scatter_dimension=0,
            tiled=True,
        ),
        lax.psum_scatter(
            widen(grad_bias_value, model_width, part * width),
            ("dp", "tensor"),
            scatter_dimension=0,
            tiled=True,
        ),
        lax.psum_scatter(grad_bias_merge, ("dp", "tensor"), scatter_dimension=0, tiled=True),
        lax.psum_scatter(grad_gain_first, ("dp", "tensor"), scatter_dimension=0, tiled=True),
        lax.psum_scatter(grad_shift_first, ("dp", "tensor"), scatter_dimension=0, tiled=True),
        lax.psum_scatter(expand_bias_term, ("dp", "tensor"), scatter_dimension=0, tiled=True),
        lax.psum_scatter(grad_bias_shrink, ("dp", "tensor"), scatter_dimension=0, tiled=True),
        lax.psum_scatter(grad_gain_second, ("dp", "tensor"), scatter_dimension=0, tiled=True),
        lax.psum_scatter(grad_shift_second, ("dp", "tensor"), scatter_dimension=0, tiled=True),
    )
    querygrad, keygrad, valuegrad, mergegrad, expandgrad, shrinkgrad = (
        lax.psum_scatter(query_local, "dp", scatter_dimension=0, tiled=True),
        lax.psum_scatter(key_local, "dp", scatter_dimension=0, tiled=True),
        lax.psum_scatter(value_local, "dp", scatter_dimension=0, tiled=True),
        lax.psum_scatter(merge_local, "dp", scatter_dimension=1, tiled=True),
        lax.psum_scatter(expand_local, "dp", scatter_dimension=0, tiled=True),
        lax.psum_scatter(shrink_local, "dp", scatter_dimension=1, tiled=True),
    )
    return (
        output,
        tokens_grad,
        querygrad,
        qbiasgrad,
        keygrad,
        valuegrad,
        vbiasgrad,
        mergegrad,
        mbiasgrad,
        fgaingrad,
        fshiftgrad,
        expandgrad,
        ebiasgrad,
        shrinkgrad,
        sbiasgrad,
        sgaingrad,
        sshiftgrad,
    )


def solution(mesh):
    return jax.shard_map(
        on_device,
        mesh=mesh,
        in_specs=(
            P(("dp", "tensor"), None),
            P("dp", "tensor"),
            P("dp", "tensor"),
            P(("dp", "tensor")),
            P("dp", "tensor"),
            P("dp", "tensor"),
            P(("dp", "tensor")),
            P("tensor", "dp"),
            P(("dp", "tensor")),
            P(("dp", "tensor")),
            P(("dp", "tensor")),
            P("dp", "tensor"),
            P(("dp", "tensor")),
            P("tensor", "dp"),
            P(("dp", "tensor")),
            P(("dp", "tensor")),
            P(("dp", "tensor")),
            P(("dp", "tensor"), None),
        ),
        out_specs=(
            P(("dp", "tensor"), None),
            P(("dp", "tensor"), None),
            P("dp", "tensor"),
            P(("dp", "tensor")),
            P("dp", "tensor"),
            P("dp", "tensor"),
            P(("dp", "tensor")),
            P("tensor", "dp"),
            P(("dp", "tensor")),
            P(("dp", "tensor")),
            P(("dp", "tensor")),
            P("dp", "tensor"),
            P(("dp", "tensor")),
            P("tensor", "dp"),
            P(("dp", "tensor")),
            P(("dp", "tensor")),
            P(("dp", "tensor")),
        ),
        check_vma=False,
    )
```

profile of v0, /device:TPU:0, one launch (start us, length us, event | category | flops | bytes accessed | tf_op | source)
XLA Modules:
  0.0 1345.0 jit_solution(11370294428568450697)
XLA Ops:
  15.5 43.1 %all-reduce.19 = (f32[768]{0:T(1024)}, f32[768]{0:T(1024)}, f32[768]{0:T(1024)S(1)}, f32[768]{0:T(1024)S(1)}, f32[768]{0:T(1024)S(1)}, /*index=5*/f32[3072]{0:T(1024)}, f32[768]{0:T(1024)}, f32[768]{0:T(1024)}) all-reduce(f32[768]{0:T(1024)S(1)} %dynamic-update-slice.4, ...), channel_id=1, replica_groups=mesh['dp'=8,'tensor'=4] {'dp','tensor'}, use_global_device_ids=true, to_apply=%add.4 | all-reduce | flops 8448 | bytes 67584
  65.9 33.4 %all_gather.62 = bf16[768,192]{1,0:T(8,128)(2,1)} all-gather(bf16[96,192]{1,0:T(8,128)(2,1)} %param.24), channel_id=1, replica_groups=mesh['dp'=8,'tensor'=4] {'dp'}, dimensions={0}, use_global_device_ids=true | all-gather | bytes 331776 | tf_op jit(solution)/shard_map/all_gather | solution.py:143
  99.2 33.3 %all_gather.65 = bf16[768,192]{1,0:T(8,128)(2,1)} all-gather(bf16[96,192]{1,0:T(8,128)(2,1)} %param.27), channel_id=1, replica_groups=mesh['dp'=8,'tensor'=4] {'dp'}, dimensions={0}, use_global_device_ids=true | all-gather | bytes 331776 | tf_op jit(solution)/shard_map/all_gather | solution.py:145
  132.5 31.3 %all_gather.64 = bf16[768,192]{1,0:T(8,128)(2,1)S(1)} all-gather(bf16[96,192]{1,0:T(8,128)(2,1)} %param.26), channel_id=1, replica_groups=mesh['dp'=8,'tensor'=4] {'dp'}, dimensions={0}, use_global_device_ids=true | all-gather | bytes 331776 | tf_op jit(solution)/shard_map/all_gather | solution.py:144
  163.8 33.0 %all_gather.67 = bf16[192,768]{0,1:T(8,128)(2,1)} all-gather(bf16[192,96]{0,1:T(8,128)(2,1)S(1)} %copy.61), channel_id=1, replica_groups=mesh['dp'=8,'tensor'=4] {'dp'}, dimensions={1}, use_global_device_ids=true | all-gather | bytes 331776 | tf_op jit(solution)/shard_map/all_gather | solution.py:146
  213.0 150.0 %while.32 = (s32[]{:T(128)}, bf16[12,512,64]{1,2,0:T(8,128)(2,1)}, f32[12,512]{1,0:T(8,128)}, s32[12]{0:T(128)S(1)}, s32[2048]{0:T(1024)S(1)}, /*index=5*/s32[1,...) while((s32[]{:T(128)}, bf16[12,512,64]{1,2,0:T(8,128)(2,1)}, ...), condition=%wide.region_3.4_spmd.clone, body=%wide.region_0.3_spmd.sunk.clone | while | flops 277872128 | bytes 33853836 | solution.py:61
  369.0 37.3 %reduce-scatter.19.cloned.1.call-done = bf16[512,768]{1,0:T(8,128)(2,1)} async-done(((bf16[2048,768]{1,0:T(8,128)(2,1)}), bf16[512,768]{1,0:T(8,128)(2,1)}) %reduce-scatter.19.cloned.1.call-update) | async-done | bytes 786448 | tf_op jit(solution)/shard_map/reduce_scatter | solution.py:192
  412.4 29.0 %all-gather.9.cloned.1.call-done = bf16[2048,768]{1,0:T(8,128)(2,1)} async-done(((bf16[512,768]{1,0:T(8,128)(2,1)}), bf16[2048,768]{1,0:T(8,128)(2,1)}) %all-gather.9.cloned.1.call-update) | async-done | bytes 3145744 | tf_op jit(solution)/shard_map/all_gather | solution.py:200
  441.3 19.0 %multiply_convert_fusion.1 = (bf16[2048,768]{1,0:T(8,128)(2,1)}, f32[2048,768]{1,0:T(8,128)}, f32[2048,768]{1,0:T(8,128)}) fusion(f32[768]{0:T(1024)S(1)} %dynamic_slice.96, bf16[2048,768]{1,0:T(8,128)(2,1)} %all-gather.9.cloned.1.call-done, bf16[768,768]{1,0:T(8,128)(2,1)} %all-gather.11.cloned.1.call-done), kind=kOutput, calls=%fused_computation.39 | convolution fusion | flops 2519728128 | bytes 20057088 | tf_op jit(solution)/shard_map/dot_general | solution.py:202
  460.3 24.9 %all-gather.13.cloned.1.call-done = bf16[768,768]{0,1:T(8,128)(2,1)} async-done(((bf16[768,96]{0,1:T(8,128)(2,1)}), bf16[768,768]{0,1:T(8,128)(2,1)}) %all-gather.13.cloned.1.call-update) | async-done | bytes 1179664 | tf_op jit(solution)/shard_map/all_gather | solution.py:148
  491.8 36.3 %reduce-scatter.21.cloned.1.call-done = bf16[512,768]{1,0:T(8,128)(2,1)} async-done(((bf16[2048,768]{1,0:T(8,128)(2,1)}), bf16[512,768]{1,0:T(8,128)(2,1)}) %reduce-scatter.21.cloned.1.call-update) | async-done | bytes 786448 | tf_op jit(solution)/shard_map/reduce_scatter | solution.py:207
  534.3 28.4 %all-gather.15.cloned.1.call-done = bf16[2048,768]{1,0:T(8,128)(2,1)} async-done(((bf16[512,768]{1,0:T(8,128)(2,1)}), bf16[2048,768]{1,0:T(8,128)(2,1)}) %all-gather.15.cloned.1.call-update) | async-done | bytes 3145744 | tf_op jit(solution)/shard_map/all_gather | solution.py:219
  562.8 11.1 fusion.50
  579.7 37.9 %reduce-scatter.23.cloned.1.call-done = bf16[512,768]{1,0:T(8,128)(2,1)} async-done(((bf16[2048,768]{1,0:T(8,128)(2,1)}), bf16[512,768]{1,0:T(8,128)(2,1)}) %reduce-scatter.23.cloned.1.call-update) | async-done | bytes 786448 | tf_op jit(solution)/shard_map/reduce_scatter | solution.py:234
  625.6 28.2 %all-gather.17.cloned.1.call-done = bf16[2048,768]{1,0:T(8,128)(2,1)} async-done(((bf16[512,768]{1,0:T(8,128)(2,1)}), bf16[2048,768]{1,0:T(8,128)(2,1)}) %all-gather.17.cloned.1.call-update) | async-done | bytes 3145744 | tf_op jit(solution)/shard_map/all_gather | solution.py:246
  658.1 228.1 %while.33 = (s32[]{:T(128)}, f32[2048,192]{0,1:T(8,128)S(1)}, f32[2048,192]{0,1:T(8,128)S(1)}, f32[12,512,64]{1,2,0:T(8,128)}, s32[12]{0:T(128)S(1)}, /*index=5*...) while((s32[]{:T(128)}, f32[2048,192]{0,1:T(8,128)S(1)}, ...), condition=%wide.region_17.18_spmd.clone, body=%wide.region_15.17_spmd.sunk.clone | while | flops 682884608 | bytes 55606196 | solution.py:111
  932.4 22.5 %reduce-scatter.37.cloned.1.call-done = f32[96,192]{1,0:T(8,128)} async-done(((f32[768,192]{1,0:T(8,128)}), f32[96,192]{1,0:T(8,128)}) %reduce-scatter.37.cloned.1.call-update) | async-done | bytes 73744
  956.6 37.7 %reduce-scatter.25.cloned.1.call-done = bf16[512,768]{1,0:T(8,128)(2,1)} async-done(((bf16[2048,768]{1,0:T(8,128)(2,1)}), bf16[512,768]{1,0:T(8,128)(2,1)}) %reduce-scatter.25.cloned.1.call-update) | async-done | bytes 786448 | tf_op jit(solution)/shard_map/reduce_scatter | solution.py:278
  997.1 41.4 %all-reduce.18 = (f32[768]{0:T(1024)S(1)}, f32[768]{0:T(1024)S(1)}, f32[768]{0:T(1024)S(1)}, f32[768]{0:T(1024)S(1)}, f32[768]{0:T(1024)S(1)}, /*index=5*/f32[76...) all-reduce(f32[768]{0:T(1024)S(1)} %dynamic-update-slice.8, ...), channel_id=1, replica_groups=mesh['dp'=8,'tensor'=4] {'dp','tensor'}, use_global_device_ids=true, to_apply=%add.8 | all-reduce | flops 9984 | bytes 79872
  1045.0 22.9 %reduce-scatter.29.cloned.1.call-done = f32[768,96]{0,1:T(8,128)} async-done(((f32[768,768]{0,1:T(8,128)}), f32[768,96]{0,1:T(8,128)}) %reduce-scatter.29.cloned.1.call-update) | async-done | bytes 294928 | tf_op jit(solution)/shard_map/reduce_scatter | solution.py:327
  1068.0 72.4 %reduce-scatter.27.cloned.1.call-done = f32[96,768]{1,0:T(8,128)} async-done(((f32[768,768]{1,0:T(8,128)}), f32[96,768]{1,0:T(8,128)}) %reduce-scatter.27.cloned.1.call-update) | async-done | bytes 294928 | tf_op jit(solution)/shard_map/reduce_scatter | solution.py:326
  1140.3 66.0 %reduce-scatter.31.cloned.1.call-done = f32[96,192]{1,0:T(8,128)} async-done(((f32[768,192]{1,0:T(8,128)}), f32[96,192]{1,0:T(8,128)}) %reduce-scatter.31.cloned.1.call-update) | async-done | bytes 73744
  1206.3 65.4 %reduce-scatter.33.cloned.1.call-done = f32[96,192]{1,0:T(8,128)} async-done(((f32[768,192]{1,0:T(8,128)}), f32[96,192]{1,0:T(8,128)}) %reduce-scatter.33.cloned.1.call-update) | async-done | bytes 73744
  1271.8 65.9 %reduce-scatter.35.cloned.1.call-done = f32[96,192]{1,0:T(8,128)} async-done(((f32[768,192]{1,0:T(8,128)}), f32[96,192]{1,0:T(8,128)}) %reduce-scatter.35.cloned.1.call-update) | async-done | bytes 73744
  (502 shorter events, 436.8 us)
Async XLA Ops:
  8.0 189.7 %all-gather.7.cloned.1.call-start = ((), (), s32[]{:S(2)}) async-start(), calls=%async_computation.10 | async-start | bytes 3932160 | tf_op jit(solution)/shard_map/all_gather | solution.py:179
  8.8 397.5 %reduce-scatter.19.cloned.1.call-start = ((), (), s32[]{:S(2)}) async-start(), calls=%async_computation.11 | async-start | bytes 3932160 | tf_op jit(solution)/shard_map/reduce_scatter | solution.py:192
  368.2 44.2 %all-gather.11.cloned.1.call-start = ((), (), s32[]{:S(2)}) async-start(), calls=%async_computation.13 | async-start | bytes 1327104 | tf_op jit(solution)/shard_map/all_gather | solution.py:147
  368.8 72.6 %all-gather.9.cloned.1.call-start = ((), (), s32[]{:S(2)}) async-start(), calls=%async_computation.12 | async-start | bytes 3932160 | tf_op jit(solution)/shard_map/all_gather | solution.py:200
  409.4 118.7 %copy-start.24 = (f32[512]{0:T(512)}, f32[512]{0:T(512)S(1)}, u32[]{:S(2)}) copy-start(f32[512]{0:T(512)S(1)} %fusion.47) | copy-start | bytes 6148
  410.8 74.3 %all-gather.13.cloned.1.call-start = ((), (), s32[]{:S(2)}) async-start(), calls=%async_computation.14 | async-start | bytes 1327104 | tf_op jit(solution)/shard_map/all_gather | solution.py:148
  411.4 116.7 %reduce-scatter.21.cloned.1.call-start = ((), (), s32[]{:S(2)}) async-start(), calls=%async_computation.15 | async-start | bytes 3932160 | tf_op jit(solution)/shard_map/reduce_scatter | solution.py:207
  491.7 71.0 %all-gather.15.cloned.1.call-start = ((), (), s32[]{:S(2)}) async-start(), calls=%async_computation.16 | async-start | bytes 3932160 | tf_op jit(solution)/shard_map/all_gather | solution.py:219
  534.1 83.5 %reduce-scatter.23.cloned.1.call-start = ((), (), s32[]{:S(2)}) async-start(), calls=%async_computation.17 | async-start | bytes 3932160 | tf_op jit(solution)/shard_map/reduce_scatter | solution.py:234
  579.7 74.1 %all-gather.17.cloned.1.call-start = ((), (), s32[]{:S(2)}) async-start(), calls=%async_computation.18 | async-start | bytes 3932160 | tf_op jit(solution)/shard_map/all_gather | solution.py:246
  625.1 329.8 %reduce-scatter.37.cloned.1.call-start = ((), (), s32[]{:S(2)}) async-start(), calls=%async_computation.25 | async-start | bytes 884736
  892.2 102.1 %reduce-scatter.25.cloned.1.call-start = ((), (), s32[]{:S(2)}) async-start(), calls=%async_computation.19 | async-start | bytes 3932160 | tf_op jit(solution)/shard_map/reduce_scatter | solution.py:278
  898.4 169.6 %reduce-scatter.29.cloned.1.call-start = ((), (), s32[]{:S(2)}) async-start(), calls=%async_computation.21 | async-start | bytes 2654208 | tf_op jit(solution)/shard_map/reduce_scatter | solution.py:327
  905.6 234.8 %reduce-scatter.27.cloned.1.call-start = ((), (), s32[]{:S(2)}) async-start(), calls=%async_computation.20 | async-start | bytes 2654208 | tf_op jit(solution)/shard_map/reduce_scatter | solution.py:326
  912.6 293.8 %reduce-scatter.31.cloned.1.call-start = ((), (), s32[]{:S(2)}) async-start(), calls=%async_computation.22 | async-start | bytes 884736
  918.7 353.1 %reduce-scatter.33.cloned.1.call-start = ((), (), s32[]{:S(2)}) async-start(), calls=%async_computation.23 | async-start | bytes 884736
  924.5 413.2 %reduce-scatter.35.cloned.1.call-start = ((), (), s32[]{:S(2)}) async-start(), calls=%async_computation.24 | async-start | bytes 884736
  929.0 68.1 %copy-start.36 = (f32[768]{0:T(1024)S(1)}, f32[768]{0:T(1024)}, u32[]{:S(2)}) copy-start(f32[768]{0:T(1024)} %get-tuple-element.407) | copy-start | bytes 9220
  929.0 68.1 %copy-start.37 = (f32[768]{0:T(1024)S(1)}, f32[768]{0:T(1024)}, u32[]{:S(2)}) copy-start(f32[768]{0:T(1024)} %get-tuple-element.411) | copy-start | bytes 9220
  929.0 68.1 %copy-start.38 = (f32[768]{0:T(1024)S(1)}, f32[768]{0:T(1024)}, u32[]{:S(2)}) copy-start(f32[768]{0:T(1024)} %get-tuple-element.412) | copy-start | bytes 9220
  929.0 114.8 %copy-start.4 = (f32[512,768]{1,0:T(8,128)S(1)}, f32[512,768]{1,0:T(8,128)}, u32[]{:S(2)}) copy-start(f32[512,768]{1,0:T(8,128)} %copy-done.3) | copy-start | bytes 4718596
  929.0 114.8 %copy-start.26 = (f32[512]{0:T(512)S(1)}, f32[512]{0:T(512)}, u32[]{:S(2)}) copy-start(f32[512]{0:T(512)} %copy-done.25) | copy-start | bytes 6148
  929.0 114.8 %copy-start.29 = (f32[768]{0:T(1024)S(1)}, f32[768]{0:T(1024)}, u32[]{:S(2)}) copy-start(f32[768]{0:T(1024)} %get-tuple-element.473) | copy-start | bytes 9220
  929.0 114.8 %copy-start.32 = (f32[512]{0:T(512)S(1)}, f32[512]{0:T(512)}, u32[]{:S(2)}) copy-start(f32[512]{0:T(512)} %copy-done.31) | copy-start | bytes 6148
  (82 other events, 730.8 us)
Sparse Core Ops, SparseCore 0:
  10.4 31.9 all-gather.6
  368.3 37.9 reduce-scatter.18
  534.2 28.5 all-gather.14
  625.2 28.5 all-gather.16
Sparse Core Ops, SparseCore 1:
  370.8 41.5 all-gather.10
  414.5 26.8 all-gather.8
  443.6 41.5 all-gather.12
  491.8 36.3 reduce-scatter.20
  579.7 37.8 reduce-scatter.22
  892.3 62.6 reduce-scatter.36
  957.3 36.9 reduce-scatter.24
  998.6 69.3 reduce-scatter.28
  1072.3 68.0 reduce-scatter.26
  1144.6 61.7 reduce-scatter.30
  1210.1 61.6 reduce-scatter.32
  1276.0 61.6 reduce-scatter.34
where the time goes:
time: 1360 us; the launch traced here: 1340 us
  waiting for transfers between devices  577 us (42%)
  matrix products  307 us (23%)
  blocking collectives  221 us (16%)
  local copies, waits for them, and re-layouts  112 us (8%)
  loops' own time  71.6 us (5%)
  other arithmetic  38.9 us (3%)
  between operations  16.2 us (1%)
    unnamed x20, waiting for transfers between devices  222 us
    unnamed x2, blocking collectives  84.6 us
    reduce_scatter x1, waiting for transfers between devices, on_device(): lax.psum_scatter(expand_local, 'dp', scatter_dimension=0, tiled=True)  72.4 us
    dot_general x24, matrix products, one(): lax.dot_general(query_rows, key_head, CONTRACT_COLUMNS, preferred_element...  70.4 us
    another operation x1, loops' own time, attend_back(): lax.scan(one, (empty, empty), jnp.arange(count * heads))  47.7 us
    dot_general x12, matrix products, one(): lax.dot_general(grad_rows, value_head, CONTRACT_COLUMNS, preferred_elemen...  47.1 us
    dot_general x12, matrix products, one(): context = jnp.dot(chance, value_head, preferred_element_type=jnp.float32)  46.9 us
    reduce_scatter x1, waiting for transfers between devices, on_device(): lax.psum_scatter(lax.dot_general(inner_low, expand_full, CONTRACT_COLUMNS...  37.9 us
  transfers between devices with their start and end apart: 16, of which 15 were waited for; matrix products, arithmetic and copies ran while one was open for 6% of the time, Pallas kernels for 0%

commit v1 on v0

--- a/solution.py
+++ b/solution.py
@@ -7,6 +7,18 @@
 EPSILON = 1e-12
 CONTRACT_ROWS = (((0,), (0,)), ((), ()))
 CONTRACT_COLUMNS = (((1,), (1,)), ((), ()))
+
+
+def doubled_up(x, axis, dim):
+    ways, here = (lax.axis_size(axis), lax.axis_index(axis))
+    grown, reach = (x, 1)
+    while reach < ways:
+        theirs = lax.ppermute(grown, axis, [(d, d ^ reach) for d in range(ways)])
+        mine_first = jnp.concatenate([grown, theirs], axis=dim)
+        theirs_first = jnp.concatenate([theirs, grown], axis=dim)
+        grown = jnp.where(here & reach == 0, mine_first, theirs_first)
+        reach = 2 * reach
+    return grown
 
 
 def normalize(values, gain, shift):
@@ -197,7 +209,7 @@
     ).astype(jnp.float32)
     mixed = tokens.astype(jnp.float32) + attended + bias_merge
     hidden = normalize(mixed, gain_first, shift_first)
-    full_hidden = lax.all_gather(hidden.astype(jnp.bfloat16), "tensor", axis=0, tiled=True)
+    full_hidden = doubled_up(hidden.astype(jnp.bfloat16), "tensor", 0)
     inner = (
         jnp.dot(full_hidden, expand_full, preferred_element_type=jnp.float32) + local_expand_bias
     )

time: 1360 us -> 1270 us (0.934)
  matrix products: 307 us -> 238 us
  local copies, waits for them, and re-layouts: 112 us -> 87.1 us
    all_gather x1, waiting for transfers between devices: 0.12 us -> 36.3 us  [on_device(): lax.all_gather(expand_proj, 'dp', axis=0, tiled=True)]
    all_gather x1 -> x0, waiting for transfers between devices: 29 us -> none  [on_device(): lax.all_gather(hidden.astype(jnp.bfloat16), 'tensor', axis=0, tiled=True)]
    while x96 -> x48, local copies, waits for them, and re-layouts: 32.7 us -> 6.31 us
    dot_general x12, matrix products: 46.9 us -> 21.7 us  [one(): context = jnp.dot(chance, value_head, preferred_element_type=jnp.float32)]
    dot_general x12, matrix products: 47.1 us -> 22.6 us  [one(): lax.dot_general(grad_rows, value_head, CONTRACT_COLUMNS, preferred_elemen...]
    dot_general x24, matrix products: 70.4 us -> 51.9 us  [one(): lax.dot_general(query_rows, key_head, CONTRACT_COLUMNS, preferred_element...]
    unnamed x20 -> x19, waiting for transfers between devices: 222 us -> 216 us
  transfers between devices with their start and end apart: 16 -> 17, of which waited for: 15 -> 15; matrix products, arithmetic and copies ran while one was open for 6% -> 7% of each run, Pallas kernels for 0% -> 0%
where the time goes in v1:
time: 1270 us; the launch traced here: 1260 us
  waiting for transfers between devices  578 us (46%)
  matrix products  238 us (19%)
  blocking collectives  222 us (17%)
  local copies, waits for them, and re-layouts  87.1 us (7%)
  loops' own time  71.4 us (6%)
  other arithmetic  46.8 us (4%)
  between operations  16.7 us (1%)
    unnamed x19, waiting for transfers between devices  216 us
    unnamed x2, blocking collectives  84.8 us
    reduce_scatter x1, waiting for transfers between devices, on_device(): lax.psum_scatter(expand_local, 'dp', scatter_dimension=0, tiled=True)  72.7 us
    dot_general x24, matrix products, one(): lax.dot_general(query_rows, key_head, CONTRACT_COLUMNS, preferred_element...  51.9 us
    another operation x1, loops' own time, attend_back(): lax.scan(one, (empty, empty), jnp.arange(count * heads))  47.5 us
    reduce_scatter x1, waiting for transfers between devices, on_device(): lax.psum_scatter(lax.dot_general(inner_low, expand_full, CONTRACT_COLUMNS...  38.1 us
    reduce_scatter x1, waiting for transfers between devices, on_device(): lax.psum_scatter((total + lax.dot_general(value_low, value_full, CONTRACT...  37.8 us
    reduce_scatter x1, waiting for transfers between devices, on_device(): lax.psum_scatter(jnp.dot(context_low, merge_full, preferred_element_type=...  37.8 us
  transfers between devices with their start and end apart: 17, of which 15 were waited for; matrix products, arithmetic and copies ran while one was open for 7% of the time, Pallas kernels for 0%

profile of v1, /device:TPU:0, one launch (start us, length us, event | category | flops | bytes accessed | tf_op | source)
XLA Modules:
  0.0 1261.2 jit_solution(12784737073061207752)
XLA Ops:
  15.5 43.1 %all-reduce.19 = (f32[768]{0:T(1024)}, f32[768]{0:T(1024)}, f32[768]{0:T(1024)S(1)}, f32[768]{0:T(1024)S(1)}, f32[768]{0:T(1024)S(1)}, /*index=5*/f32[3072]{0:T(1024)}, f32[768]{0:T(1024)}, f32[768]{0:T(1024)}) all-reduce(f32[768]{0:T(1024)S(1)} %dynamic-update-slice.4, ...), channel_id=1, replica_groups=mesh['dp'=8,'tensor'=4] {'dp','tensor'}, use_global_device_ids=true, to_apply=%add.4 | all-reduce | flops 8448 | bytes 67584
  65.9 33.2 %all_gather.64 = bf16[192,768]{0,1:T(8,128)(2,1)} all-gather(bf16[192,96]{0,1:T(8,128)(2,1)S(1)} %copy.61), channel_id=1, replica_groups=mesh['dp'=8,'tensor'=4] {'dp'}, dimensions={1}, use_global_device_ids=true | all-gather | bytes 331776 | tf_op jit(solution)/shard_map/all_gather | solution.py:158
  99.0 33.3 %all_gather.59 = bf16[768,192]{1,0:T(8,128)(2,1)} all-gather(bf16[96,192]{1,0:T(8,128)(2,1)} %param.24), channel_id=1, replica_groups=mesh['dp'=8,'tensor'=4] {'dp'}, dimensions={0}, use_global_device_ids=true | all-gather | bytes 331776 | tf_op jit(solution)/shard_map/all_gather | solution.py:155
  132.3 31.5 %all_gather.61 = bf16[768,192]{1,0:T(8,128)(2,1)S(1)} all-gather(bf16[96,192]{1,0:T(8,128)(2,1)} %param.26), channel_id=1, replica_groups=mesh['dp'=8,'tensor'=4] {'dp'}, dimensions={0}, use_global_device_ids=true | all-gather | bytes 331776 | tf_op jit(solution)/shard_map/all_gather | solution.py:156
  163.8 33.2 %all_gather.62 = bf16[768,192]{1,0:T(8,128)(2,1)} all-gather(bf16[96,192]{1,0:T(8,128)(2,1)} %param.27), channel_id=1, replica_groups=mesh['dp'=8,'tensor'=4] {'dp'}, dimensions={0}, use_global_device_ids=true | all-gather | bytes 331776 | tf_op jit(solution)/shard_map/all_gather | solution.py:157
  213.2 106.4 %while.32 = (s32[]{:T(128)}, bf16[12,512,64]{1,2,0:T(8,128)(2,1)}, f32[12,512]{1,0:T(8,128)}, s32[12]{0:T(128)S(1)}, s32[2048]{0:T(1024)S(1)}, /*index=5*/s32[1,...) while((s32[]{:T(128)}, bf16[12,512,64]{1,2,0:T(8,128)(2,1)}, ...), condition=%wide.region_3.4_spmd.clone, body=%wide.region_0.3_spmd.sunk.clone | while | flops 277872128 | bytes 17076092 | solution.py:73
  325.0 37.8 %reduce-scatter.19.cloned.1.call-done = bf16[512,768]{1,0:T(8,128)(2,1)} async-done(((bf16[2048,768]{1,0:T(8,128)(2,1)}), bf16[512,768]{1,0:T(8,128)(2,1)}) %reduce-scatter.19.cloned.1.call-update) | async-done | bytes 786448 | tf_op jit(solution)/shard_map/reduce_scatter | solution.py:204
  372.4 36.3 %all-gather.8.cloned.1.call-done = bf16[768,768]{1,0:T(8,128)(2,1)} async-done(((bf16[96,768]{1,0:T(8,128)(2,1)}), bf16[768,768]{1,0:T(8,128)(2,1)}) %all-gather.8.cloned.1.call-update) | async-done | bytes 1179664 | tf_op jit(solution)/shard_map/all_gather | solution.py:159
  408.6 21.0 %multiply_convert_fusion.1 = (bf16[2048,768]{1,0:T(8,128)(2,1)}, f32[2048,768]{1,0:T(8,128)}, f32[2048,768]{1,0:T(8,128)}) fusion(f32[768]{0:T(1024)S(1)} %dynamic_slice.96, bf16[768,768]{1,0:T(8,128)(2,1)} %all-gather.8.cloned.1.call-done, bf16[1024,768]{1,0:T(8,128)(2,1)} %collective-permute-done.1, bf16[1024,768]{1,0:T(8,128)(2,1)} %maximum_select_fusion.1, ...), kind=kOutput, calls=%fused_computation.39 | convolution fusion | flops 2533883904 | bytes 20057088 | tf_op jit(solution)/shard_map/dot_general | solution.py:214
  429.6 21.3 %all-gather.10.cloned.1.call-done = bf16[768,768]{0,1:T(8,128)(2,1)} async-done(((bf16[768,96]{0,1:T(8,128)(2,1)}), bf16[768,768]{0,1:T(8,128)(2,1)}) %all-gather.10.cloned.1.call-update) | async-done | bytes 1179664 | tf_op jit(solution)/shard_map/all_gather | solution.py:160
  457.6 36.5 %reduce-scatter.21.cloned.1.call-done = bf16[512,768]{1,0:T(8,128)(2,1)} async-done(((bf16[2048,768]{1,0:T(8,128)(2,1)}), bf16[512,768]{1,0:T(8,128)(2,1)}) %reduce-scatter.21.cloned.1.call-update) | async-done | bytes 786448 | tf_op jit(solution)/shard_map/reduce_scatter | solution.py:219
  500.4 28.4 %all-gather.12.cloned.1.call-done = bf16[2048,768]{1,0:T(8,128)(2,1)} async-done(((bf16[512,768]{1,0:T(8,128)(2,1)}), bf16[2048,768]{1,0:T(8,128)(2,1)}) %all-gather.12.cloned.1.call-update) | async-done | bytes 3145744 | tf_op jit(solution)/shard_map/all_gather | solution.py:231
  546.4 38.1 %reduce-scatter.23.cloned.1.call-done = bf16[512,768]{1,0:T(8,128)(2,1)} async-done(((bf16[2048,768]{1,0:T(8,128)(2,1)}), bf16[512,768]{1,0:T(8,128)(2,1)}) %reduce-scatter.23.cloned.1.call-update) | async-done | bytes 786448 | tf_op jit(solution)/shard_map/reduce_scatter | solution.py:246
  592.4 28.2 %all-gather.14.cloned.1.call-done = bf16[2048,768]{1,0:T(8,128)(2,1)} async-done(((bf16[512,768]{1,0:T(8,128)(2,1)}), bf16[2048,768]{1,0:T(8,128)(2,1)}) %all-gather.14.cloned.1.call-update) | async-done | bytes 3145744 | tf_op jit(solution)/shard_map/all_gather | solution.py:258
  625.0 178.2 %while.33 = (s32[]{:T(128)}, f32[2048,192]{0,1:T(8,128)S(1)}, f32[2048,192]{0,1:T(8,128)S(1)}, f32[12,512,64]{1,2,0:T(8,128)}, s32[12]{0:T(128)S(1)}, /*index=5*...) while((s32[]{:T(128)}, f32[2048,192]{0,1:T(8,128)S(1)}, ...), condition=%wide.region_17.18_spmd.clone, body=%wide.region_15.17_spmd.sunk.clone | while | flops 682884608 | bytes 38828452 | solution.py:123
  822.8 8.0 fusion.36
  852.5 17.8 %reduce-scatter.37.cloned.1.call-done = f32[96,192]{1,0:T(8,128)} async-done(((f32[768,192]{1,0:T(8,128)}), f32[96,192]{1,0:T(8,128)}) %reduce-scatter.37.cloned.1.call-update) | async-done | bytes 73744
  871.9 37.8 %reduce-scatter.25.cloned.1.call-done = bf16[512,768]{1,0:T(8,128)(2,1)} async-done(((bf16[2048,768]{1,0:T(8,128)(2,1)}), bf16[512,768]{1,0:T(8,128)(2,1)}) %reduce-scatter.25.cloned.1.call-update) | async-done | bytes 786448 | tf_op jit(solution)/shard_map/reduce_scatter | solution.py:290
  912.5 41.7 %all-reduce.18 = (f32[768]{0:T(1024)S(1)}, f32[768]{0:T(1024)S(1)}, f32[768]{0:T(1024)S(1)}, f32[768]{0:T(1024)S(1)}, f32[768]{0:T(1024)S(1)}, /*index=5*/f32[76...) all-reduce(f32[768]{0:T(1024)S(1)} %dynamic-update-slice.8, ...), channel_id=1, replica_groups=mesh['dp'=8,'tensor'=4] {'dp','tensor'}, use_global_device_ids=true, to_apply=%add.8 | all-reduce | flops 9984 | bytes 79872
  960.7 23.2 %reduce-scatter.29.cloned.1.call-done = f32[768,96]{0,1:T(8,128)} async-done(((f32[768,768]{0,1:T(8,128)}), f32[768,96]{0,1:T(8,128)}) %reduce-scatter.29.cloned.1.call-update) | async-done | bytes 294928 | tf_op jit(solution)/shard_map/reduce_scatter | solution.py:339
  983.8 72.7 %reduce-scatter.27.cloned.1.call-done = f32[96,768]{1,0:T(8,128)} async-done(((f32[768,768]{1,0:T(8,128)}), f32[96,768]{1,0:T(8,128)}) %reduce-scatter.27.cloned.1.call-update) | async-done | bytes 294928 | tf_op jit(solution)/shard_map/reduce_scatter | solution.py:338
  1056.5 65.8 %reduce-scatter.31.cloned.1.call-done = f32[96,192]{1,0:T(8,128)} async-done(((f32[768,192]{1,0:T(8,128)}), f32[96,192]{1,0:T(8,128)}) %reduce-scatter.31.cloned.1.call-update) | async-done | bytes 73744
  1122.3 65.4 %reduce-scatter.35.cloned.1.call-done = f32[96,192]{1,0:T(8,128)} async-done(((f32[768,192]{1,0:T(8,128)}), f32[96,192]{1,0:T(8,128)}) %reduce-scatter.35.cloned.1.call-update) | async-done | bytes 73744
  1187.7 65.7 %reduce-scatter.33.cloned.1.call-done = f32[96,192]{1,0:T(8,128)} async-done(((f32[768,192]{1,0:T(8,128)}), f32[96,192]{1,0:T(8,128)}) %reduce-scatter.33.cloned.1.call-update) | async-done | bytes 73744
  (463 shorter events, 353.4 us)
Async XLA Ops:
  8.0 189.9 %all-gather.6.cloned.1.call-start = ((), (), s32[]{:S(2)}) async-start(), calls=%async_computation.10 | async-start | bytes 3932160 | tf_op jit(solution)/shard_map/all_gather | solution.py:191
  8.8 354.0 %reduce-scatter.19.cloned.1.call-start = ((), (), s32[]{:S(2)}) async-start(), calls=%async_computation.11 | async-start | bytes 3932160 | tf_op jit(solution)/shard_map/reduce_scatter | solution.py:204
  324.8 83.8 %all-gather.8.cloned.1.call-start = ((), (), s32[]{:S(2)}) async-start(), calls=%async_computation.12 | async-start | bytes 1327104 | tf_op jit(solution)/shard_map/all_gather | solution.py:159
  367.0 2.4 collective-permute-start
  367.1 83.9 %all-gather.10.cloned.1.call-start = ((), (), s32[]{:S(2)}) async-start(), calls=%async_computation.13 | async-start | bytes 1327104 | tf_op jit(solution)/shard_map/all_gather | solution.py:160
  371.2 37.4 %collective-permute-start.1 = (bf16[1024,768]{1,0:T(8,128)(2,1)}, bf16[1024,768]{1,0:T(8,128)(2,1)}, u32[]{:S(2)}, u32[]{:S(2)}) collective-permute-start(bf16[1024,768]{1,0:T(8,128)(2,1)} %maximum_select_fusion.1), channel_id=1, source_target_pairs={{0,2},{1,3},{2,0},{3,1},{4,6},{5,7},{6,4},{7,5},{8,10},{9,11},{10,... | collective-permute-start | bytes 4718600 | tf_op jit(solution)/shard_map/ppermute | solution.py:16
  371.5 122.6 %reduce-scatter.21.cloned.1.call-start = ((), (), s32[]{:S(2)}) async-start(), calls=%async_computation.14 | async-start | bytes 3932160 | tf_op jit(solution)/shard_map/reduce_scatter | solution.py:219
  457.6 71.2 %all-gather.12.cloned.1.call-start = ((), (), s32[]{:S(2)}) async-start(), calls=%async_computation.15 | async-start | bytes 3932160 | tf_op jit(solution)/shard_map/all_gather | solution.py:231
  500.1 84.4 %reduce-scatter.23.cloned.1.call-start = ((), (), s32[]{:S(2)}) async-start(), calls=%async_computation.16 | async-start | bytes 3932160 | tf_op jit(solution)/shard_map/reduce_scatter | solution.py:246
  546.4 74.3 %all-gather.14.cloned.1.call-start = ((), (), s32[]{:S(2)}) async-start(), calls=%async_computation.17 | async-start | bytes 3932160 | tf_op jit(solution)/shard_map/all_gather | solution.py:258
  592.0 278.3 %reduce-scatter.37.cloned.1.call-start = ((), (), s32[]{:S(2)}) async-start(), calls=%async_computation.24 | async-start | bytes 884736
  807.6 102.1 %reduce-scatter.25.cloned.1.call-start = ((), (), s32[]{:S(2)}) async-start(), calls=%async_computation.18 | async-start | bytes 3932160 | tf_op jit(solution)/shard_map/reduce_scatter | solution.py:290
  815.5 168.4 %reduce-scatter.29.cloned.1.call-start = ((), (), s32[]{:S(2)}) async-start(), calls=%async_computation.20 | async-start | bytes 2654208 | tf_op jit(solution)/shard_map/reduce_scatter | solution.py:339
  822.7 233.8 %reduce-scatter.27.cloned.1.call-start = ((), (), s32[]{:S(2)}) async-start(), calls=%async_computation.19 | async-start | bytes 2654208 | tf_op jit(solution)/shard_map/reduce_scatter | solution.py:338
  830.8 291.5 %reduce-scatter.31.cloned.1.call-start = ((), (), s32[]{:S(2)}) async-start(), calls=%async_computation.21 | async-start | bytes 884736
  836.8 350.9 %reduce-scatter.35.cloned.1.call-start = ((), (), s32[]{:S(2)}) async-start(), calls=%async_computation.23 | async-start | bytes 884736
  842.7 410.7 %reduce-scatter.33.cloned.1.call-start = ((), (), s32[]{:S(2)}) async-start(), calls=%async_computation.22 | async-start | bytes 884736
  849.0 63.5 %copy-start.36 = (f32[768]{0:T(1024)S(1)}, f32[768]{0:T(1024)}, u32[]{:S(2)}) copy-start(f32[768]{0:T(1024)} %get-tuple-element.407) | copy-start | bytes 9220
  849.0 63.5 %copy-start.37 = (f32[768]{0:T(1024)S(1)}, f32[768]{0:T(1024)}, u32[]{:S(2)}) copy-start(f32[768]{0:T(1024)} %get-tuple-element.411) | copy-start | bytes 9220
  849.1 63.5 %copy-start.38 = (f32[768]{0:T(1024)S(1)}, f32[768]{0:T(1024)}, u32[]{:S(2)}) copy-start(f32[768]{0:T(1024)} %get-tuple-element.412) | copy-start | bytes 9220
  849.1 110.4 %copy-start.2 = (f32[512,768]{1,0:T(8,128)S(1)}, f32[512,768]{1,0:T(8,128)}, u32[]{:S(2)}) copy-start(f32[512,768]{1,0:T(8,128)} %copy-done.1) | copy-start | bytes 4718596
  849.1 110.4 %copy-start.26 = (f32[512]{0:T(512)S(1)}, f32[512]{0:T(512)}, u32[]{:S(2)}) copy-start(f32[512]{0:T(512)} %copy-done.25) | copy-start | bytes 6148
  849.1 110.4 %copy-start.29 = (f32[768]{0:T(1024)S(1)}, f32[768]{0:T(1024)}, u32[]{:S(2)}) copy-start(f32[768]{0:T(1024)} %get-tuple-element.473) | copy-start | bytes 9220
  849.1 110.4 %copy-start.32 = (f32[512]{0:T(512)S(1)}, f32[512]{0:T(512)}, u32[]{:S(2)}) copy-start(f32[512]{0:T(512)} %copy-done.31) | copy-start | bytes 6148
  (62 other events, 701.7 us)
Sparse Core Ops, SparseCore 0:
  10.4 31.9 all-gather.5
  324.9 37.8 reduce-scatter.18
  457.6 36.4 reduce-scatter.20
  500.2 28.5 all-gather.11
  546.5 37.9 reduce-scatter.22
  592.1 28.5 all-gather.13
Sparse Core Ops, SparseCore 1:
  367.2 41.4 all-gather.7
  410.9 40.0 all-gather.9
  807.7 62.6 reduce-scatter.36
  872.8 36.8 reduce-scatter.24
  914.2 69.6 reduce-scatter.28
  988.3 68.1 reduce-scatter.26
  1060.6 61.6 reduce-scatter.30
  1126.1 61.6 reduce-scatter.34
  1191.8 61.5 reduce-scatter.32
